TPU v7x, 32 devices: a whole 2x2x4 slice. The times are simulated.
32 devices in a mesh: req: 8 (over z, x), grp: 4 (over y, core).
Axes of the slice: x: 2, y: 2, z: 4, core: 2. Of those that a mesh axis runs over, the one named last changes fastest.
Arguments:
- hidden: bfloat16 [256, 16, 1024], P(('grp', 'req')), parts along dimension 0, may hold values from -6 to 6
- norm_gain: float32 [1024], replicated, may hold values from 0.1 to 1.9
- in_weight: bfloat16 [1024, 4096], replicated, may hold values from -0.1875 to 0.1875
- conv_weight: float32 [4, 2048], P(None, 'req'), may hold values from -3 to 3
- conv_bias: float32 [2048], P('req'), may hold values from -3 to 3
- x_weight: bfloat16 [2048, 160], P('req'), may hold values from -0.125 to 0.125
- step_weight: bfloat16 [128, 2048], P(None, 'req'), may hold values from -0.5 to 0.5
- step_bias: float32 [2048], P('req'), may hold values from -5 to -1
- log_decay: float32 [16, 2048], P(None, 'req'), may hold values from -0.7 to 2.8
- skip_gain: float32 [2048], P('req'), may hold values from 0.5 to 1.5
- out_weight: bfloat16 [2048, 1024], replicated, may hold values from -0.125 to 0.125
- old_states: float32 [256, 16, 2048], P(('grp', 'req')), parts along dimension 0, may hold values from -3 to 3
- old_edges: bfloat16 [256, 3, 2048], P(('grp', 'req')), parts along dimension 0, may hold values from -6 to 6
- anchor: int32 [256], P('grp'), parts along dimension 0, may hold values from 0 to 63, each once
- fresh_flag: int32 [256], P('grp'), parts along dimension 0, may hold values 0 or 1
- accepted: int32 [256], P('grp'), parts along dimension 0, may hold values from 1 to 16
- request_ages: int32 [256], P('grp'), parts along dimension 0, may hold values from 0 to 7
Outputs:
- layer_out: bfloat16 [256, 16, 1024], P(('grp', 'req')), parts along dimension 0
- new_states: float32 [256, 16, 2048], P(('grp', 'req')), parts along dimension 0
There are 4 independent parts, one for each index of `grp`. A program takes and returns all parts, laid end to end along the dimension named above; an argument that names none is the same for every part. Nothing has to cross between parts.
Inputs may be any that keep to these rules, and one draw needn't show every extreme that they name: Every old slot is the anchor of exactly one request.
All inputs are finite; a program needn't handle non-finite values.
Results may differ from a plain program's by a relative error of at most 0.0091.
Values may be sent and summed in bfloat16 or wider, within the bound.
No kernel may reach another device: no remote copies, remote signals or barrier semaphores. Data moves between devices by JAX's collectives and lax.ppermute only.
A program may use at most 128 MiB of HBM per device.

v0:
```python
import jax
import jax.numpy as jnp
from jax import lax
from jax.sharding import PartitionSpec as P

EPS = 1e-05


def rms_normed(values_in, norm_gain):
    values = values_in.astype(jnp.float32)
    factor = lax.rsqrt(jnp.mean(values * values, axis=-1, keepdims=True) + EPS)
    return (values * factor * norm_gain).astype(jnp.bfloat16)


def on_device(
    hidden,
    norm_gain,
    in_weight,
    conv_weight,
    conv_bias,
    x_weight,
    step_weight,
    step_bias,
    log_decay,
    skip_gain,
    out_weight,
    old_states,
    old_edges,
    anchor,
    fresh_flag,
    accepted,
    request_ages,
):
    local_reqs, draft_len, width = hidden.shape
    inner_width = out_weight.shape[0]
    channels = conv_weight.shape[1]
    state_size = log_decay.shape[0]
    low_rank = step_weight.shape[0]
    span = old_edges.shape[1]
    state_lead = jnp.swapaxes(old_states, 0, 1)
    edge_lead = jnp.swapaxes(old_edges.astype(jnp.float32), 0, 1)
    moved_states, moved_edges = (
        lax.all_to_all(state_lead, "req", split_axis=2, concat_axis=1, tiled=True),
        lax.all_to_all(edge_lead, "req", split_axis=2, concat_axis=1, tiled=True),
    )
    token_major = jnp.swapaxes(hidden, 0, 1).reshape(draft_len * local_reqs, width)
    normed = rms_normed(token_major, norm_gain)
    projected = jnp.dot(normed, in_weight, preferred_element_type=jnp.float32).astype(jnp.bfloat16)
    projected = jnp.moveaxis(projected.reshape(draft_len, local_reqs, 2, inner_width), 2, 0)
    grouped = lax.all_to_all(projected, "req", split_axis=3, concat_axis=2, tiled=True)
    all_reqs = grouped.shape[2]
    inner_part = grouped[0]
    gate_part = grouped[1]
    keep_state = (1 - fresh_flag).astype(jnp.float32)
    start_state = jnp.take(moved_states, anchor, axis=1) * keep_state[None, :, None]
    edges = jnp.take(moved_edges, anchor, axis=1)
    distance = span - jnp.arange(span, dtype=jnp.int32)
    usable = (distance[:, None] <= request_ages[None, :]) & (fresh_flag[None, :] == 0)
    history = jnp.where(usable[:, :, None], edges, jnp.zeros((), jnp.float32))
    sequence = jnp.concatenate([history, inner_part.astype(jnp.float32)], axis=0)
    running = conv_bias + conv_weight[0] * sequence[0:draft_len]
    for offset in range(1, conv_weight.shape[0]):
        running = running + conv_weight[offset] * sequence[offset : offset + draft_len]
    conv_out = jax.nn.silu(running).astype(jnp.bfloat16)
    conv_rows = conv_out.reshape(draft_len * all_reqs, channels)
    partial_value = jnp.dot(conv_rows, x_weight, preferred_element_type=jnp.float32)
    mixed_rows = lax.psum(partial_value, "req").astype(jnp.bfloat16)
    flat = all_reqs * channels
    step_sizes = jax.nn.softplus(
        jnp.dot(mixed_rows[:, :low_rank], step_weight, preferred_element_type=jnp.float32)
        + step_bias
    )
    step_sizes = step_sizes.reshape(draft_len, flat)
    coeffs = (
        mixed_rows[:, low_rank:].astype(jnp.float32).reshape(draft_len, all_reqs, 2 * state_size)
    )
    b_coeff = coeffs[:, :, :state_size]
    c_coeff = coeffs[:, :, state_size:]
    inputs = conv_out.astype(jnp.float32)
    flat_inputs = inputs.reshape(draft_len, flat)
    decay = jnp.broadcast_to(
        (-jnp.exp(log_decay))[:, None, :], (state_size, all_reqs, channels)
    ).reshape(state_size, flat)
    start_flat = start_state.reshape(state_size, flat)

    def spread(per_token):
        return jnp.broadcast_to(
            jnp.swapaxes(per_token, 0, 1)[:, :, None], (state_size, all_reqs, channels)
        ).reshape(state_size, flat)

    def advance(carried, sliced):
        current, chosen = carried
        step_delta, step_b, step_c, step_input, step_index = sliced
        factor = jnp.exp(step_delta[None, :] * decay)
        current = factor * current + (step_delta * step_input)[None, :] * spread(step_b)
        result = jnp.sum(spread(step_c) * current, axis=0)
        picked = jnp.broadcast_to(
            (accepted == step_index + 1)[:, None], (all_reqs, channels)
        ).reshape(flat)
        chosen = jnp.where(picked[None, :], current, chosen)
        return ((current, chosen), result)

    sliced = (step_sizes, b_coeff, c_coeff, flat_inputs, jnp.arange(draft_len, dtype=jnp.int32))
    (final_state, chosen), outputs = lax.scan(advance, (start_flat, start_flat), sliced)
    outputs = outputs.reshape(draft_len, all_reqs, channels)
    gated_rows = (
        (outputs + skip_gain * inputs) * jax.nn.silu(gate_part.astype(jnp.float32))
    ).astype(jnp.bfloat16)
    returned = lax.all_to_all(gated_rows, "req", split_axis=1, concat_axis=2, tiled=True)
    layer_out = jnp.dot(
        returned.reshape(draft_len * local_reqs, inner_width),
        out_weight,
        preferred_element_type=jnp.float32,
    ).astype(jnp.bfloat16)
    layer_out = jnp.swapaxes(layer_out.reshape(draft_len, local_reqs, width), 0, 1)
    owned = lax.all_to_all(
        chosen.reshape(state_size, all_reqs, channels),
        "req",
        split_axis=1,
        concat_axis=2,
        tiled=True,
    )
    return (layer_out, jnp.swapaxes(owned, 0, 1))


def solution(mesh):
    return jax.shard_map(
        on_device,
        mesh=mesh,
        in_specs=(
            P(("grp", "req"), None, None),
            P(),
            P(),
            P(None, "req"),
            P("req"),
            P("req", None),
            P(None, "req"),
            P("req"),
            P(None, "req"),
            P("req"),
            P(),
            P(("grp", "req"), None, None),
            P(("grp", "req"), None, None),
            P("grp"),
            P("grp"),
            P("grp"),
            P("grp"),
        ),
        out_specs=(P(("grp", "req"), None, None), P(("grp", "req"), None, None)),
        check_vma=False,
    )
```

profile of v0, /device:TPU:0, one launch (start us, length us, event | category | flops | bytes accessed | tf_op | source)
XLA Modules:
  0.0 369.8 jit_solution(14479661632174473123)
XLA Ops:
  0.7 4.0 %copy.100 = f32[8,3,2048]{0,1,2:T(4,128)} copy(bf16[8,3,2048]{2,0,1:T(8,128)(2,1)} %param.31) | data formatting | bytes 294912 | tf_op jit(solution)/shard_map/transpose | solution.py:41
  4.7 3.9 %bitcast_bitcast_fusion.2 = f32[2048,3,8]{2,1,0:T(4,128)} fusion(f32[8,3,2048]{0,1,2:T(4,128)} %copy.100), kind=kLoop, calls=%fused_computation.72 | loop fusion | bytes 393216
  8.6 5.1 %reshape.188 = f32[8,1,6144]{2,1,0:T(1,128)} reshape(f32[2048,3,8]{2,1,0:T(4,128)} %bitcast_bitcast_fusion.2) | data formatting | bytes 393216
  13.7 7.3 %all-to-all-start.1 = ((f32[8,1,6144]{2,1,0:T(1,128)}), f32[8,1,6144]{2,1,0:T(1,128)S(1)}, u32[]{:S(2)}, u32[]{:S(2)}) async-start(f32[8,1,6144]{2,1,0:T(1,128)} %reshape.188), calls=%async_computation.1 | async-start | bytes 393216 | tf_op jit(solution)/shard_map/all_to_all | solution.py:44
  20.9 4.7 %copy.94 = f32[8,16,2048]{1,0,2:T(8,128)} copy(f32[8,16,2048]{2,1,0:T(8,128)S(1)} %copy-done.3) | data formatting | bytes 2097152 | tf_op args[11]
  26.0 4.8 %convolution_convert_fusion = bf16[128,4096]{1,0:T(8,128)(2,1)S(1)} fusion(bf16[1024,4096]{1,0:T(8,128)(2,1)} %param.21, f32[1024]{0:T(1024)S(1)} %copy-done.4, f32[128]{0:T(128)S(1)} %rsqrt.12, bf16[8,16,1024]{2,1,0:T(8,128)(2,1)S(1)} %copy-done.2), kind=kOutput, calls=%fused_computation.11 | convolution fusion | flops 1074790400 | bytes 9703936 | tf_op jit(solution)/shard_map/dot_general | solution.py:48
  30.8 8.9 %copy.103 = bf16[16,8,2,2048]{0,1,2,3:T(8,128)(2,1)} copy(bf16[16,8,2,2048]{3,1,2,0:T(8,128)(2,1)S(1)} %bitcast.169) | data formatting | bytes 2097152 | tf_op jit(solution)/shard_map/reshape | solution.py:49
  39.6 7.5 %bitcast_bitcast_fusion = bf16[2048,2,8,16]{3,2,1,0:T(8,128)(2,1)} fusion(bf16[16,8,2,2048]{0,1,2,3:T(8,128)(2,1)} %copy.103), kind=kLoop, calls=%fused_computation.70 | loop fusion | bytes 2097152
  47.1 5.8 %bitcast_bitcast_fusion.1 = f32[2048,8,16]{2,1,0:T(8,128)} fusion(f32[8,16,2048]{1,0,2:T(8,128)} %copy.94), kind=kLoop, calls=%fused_computation.71 | loop fusion | bytes 2097152
  52.9 8.1 %reshape.184 = f32[8,1,32768]{2,1,0:T(1,128)} reshape(f32[2048,8,16]{2,1,0:T(8,128)} %bitcast_bitcast_fusion.1) | data formatting | bytes 2097152
  61.1 6.0 %all-to-all-start = ((f32[8,1,32768]{2,1,0:T(1,128)}), f32[8,1,32768]{2,1,0:T(1,128)S(1)}, u32[]{:S(2)}, u32[]{:S(2)}) async-start(f32[8,1,32768]{2,1,0:T(1,128)} %reshape.184), calls=%async_computation | async-start | bytes 2097152 | tf_op jit(solution)/shard_map/all_to_all | solution.py:43
  67.3 11.3 %reshape.186 = bf16[8,2,32768]{2,1,0:T(2,128)(2,1)} reshape(bf16[2048,2,8,16]{3,2,1,0:T(8,128)(2,1)} %bitcast_bitcast_fusion) | data formatting | bytes 2097152
  80.5 4.7 %reshape.189 = f32[2048,3,8]{2,1,0:T(4,128)} reshape(f32[8,6144]{1,0:T(8,128)S(1)} %reduce.3) | data formatting | bytes 393216
  85.2 3.5 copy.101
  89.6 2.9 all-to-all-done
  92.5 3.7 %all-to-all-start.2 = ((bf16[8,2,32768]{2,1,0:T(2,128)(2,1)}), bf16[8,2,32768]{2,1,0:T(2,128)(2,1)S(1)}, u32[]{:S(2)}, u32[]{:S(2)}) async-start(bf16[8,2,32768]{2,1,0:T(2,128)(2,1)} %reshape.186), calls=%async_computation.2 | async-start | bytes 2097152 | tf_op jit(solution)/shard_map/all_to_all | solution.py:50
  96.3 3.1 reduce.2
  99.4 6.1 %reshape.185 = f32[2048,8,16]{2,1,0:T(8,128)} reshape(f32[8,32768]{1,0:T(8,128)S(1)} %reduce.2) | data formatting | bytes 2097152
  105.5 5.4 %copy.96 = f32[16,8,8,256]{3,2,1,0:T(8,128)S(1)} copy(f32[16,8,8,256]{0,2,3,1:T(8,128)} %bitcast.155) | data formatting | bytes 2097152 | tf_op jit(solution)/shard_map/all_to_all | solution.py:43
  112.4 9.5 %all-to-all-done.2 = bf16[8,2,32768]{2,1,0:T(2,128)(2,1)S(1)} async-done(((bf16[8,2,32768]{2,1,0:T(2,128)(2,1)}), bf16[8,2,32768]{2,1,0:T(2,128)(2,1)S(1)}, u32[]{:S(2)}, u32[]{:S(2)}) %all-to-all-start.2) | async-done | bytes 1048608 | tf_op jit(solution)/shard_map/all_to_all | solution.py:50
  121.9 7.6 %reshape.187 = bf16[2048,2,8,16]{3,2,1,0:T(8,128)(2,1)} reshape(bf16[8,2,32768]{2,1,0:T(2,128)(2,1)S(1)} %all-to-all-done.2) | data formatting | bytes 2097152
  129.5 8.9 %copy.104 = bf16[2,16,8,8,256]{4,2,3,1,0:T(8,128)(2,1)S(1)} copy(bf16[2,16,8,8,256]{1,2,0,4,3:T(8,128)(2,1)} %bitcast.156) | data formatting | bytes 2097152 | tf_op jit(solution)/shard_map/all_to_all | solution.py:50
  140.2 43.6 %all-reduce.1 = bf16[1024,160]{0,1:T(8,128)(2,1)} all-reduce(f32[1024,160]{0,1:T(8,128)S(1)} %fusion.29), channel_id=1, replica_groups=mesh['req'=8,'grp'=4] {'req'}, use_global_device_ids=true, to_apply=%region_1.2 | all-reduce | flops 163840 | bytes 983040 | tf_op jit(solution)/shard_map/psum | solution.py:67
  184.7 2.7 compare_select_fusion
  187.4 2.4 reshape.145
  191.2 132.7 %while.15 = (s32[]{:T(128)}, f32[16,16384]{1,0:T(8,128)S(1)}, f32[16,16384]{1,0:T(8,128)S(1)}, f32[16,16384]{1,0:T(8,128)}, f32[16,16384]{1,0:T(8,128)}, /*index...) while((s32[]{:T(128)}, f32[16,16384]{1,0:T(8,128)S(1)}, ...), condition=%wide.region_4.5_spmd.clone, body=%wide.region_2.4_spmd.clone.sunk | while | flops 1835075 | bytes 18522676 | solution.py:104
  192.9 1.3 constant_dynamic-slice_fusion.6
  197.6 1.9 dynamic_update_slice.6
  201.2 1.3 constant_dynamic-slice_fusion.6
  205.9 1.9 dynamic_update_slice.6
  209.5 1.3 constant_dynamic-slice_fusion.6
  214.2 1.9 dynamic_update_slice.6
  217.8 1.3 constant_dynamic-slice_fusion.6
  222.5 1.9 dynamic_update_slice.6
  226.1 1.3 constant_dynamic-slice_fusion.6
  230.7 1.9 dynamic_update_slice.6
  234.3 1.3 constant_dynamic-slice_fusion.6
  239.0 1.9 dynamic_update_slice.6
  242.6 1.3 constant_dynamic-slice_fusion.6
  247.3 1.9 dynamic_update_slice.6
  250.9 1.3 constant_dynamic-slice_fusion.6
  255.6 1.9 dynamic_update_slice.6
  259.2 1.3 constant_dynamic-slice_fusion.6
  263.9 1.9 dynamic_update_slice.6
  267.5 1.3 constant_dynamic-slice_fusion.6
  272.2 1.9 dynamic_update_slice.6
  275.8 1.3 constant_dynamic-slice_fusion.6
  280.5 1.9 dynamic_update_slice.6
  288.8 1.9 dynamic_update_slice.6
  292.4 1.3 constant_dynamic-slice_fusion.6
  297.1 1.9 dynamic_update_slice.6
  300.7 1.3 constant_dynamic-slice_fusion.6
  305.4 1.9 dynamic_update_slice.6
  313.7 1.9 dynamic_update_slice.6
  317.3 1.3 constant_dynamic-slice_fusion.6
  322.0 1.9 dynamic_update_slice.6
  323.9 1.5 copy.127
  325.5 1.5 fusion.16
  328.1 3.5 all-to-all-start.3
  332.7 9.4 %all-to-all-done.3 = bf16[16,64,256]{2,0,1:T(8,128)(2,1)S(1)} async-done(((bf16[16,64,256]{2,0,1:T(8,128)(2,1)}), bf16[16,64,256]{2,0,1:T(8,128)(2,1)S(1)}, u32[]{:S(2)}, u32[]{:S(2)}) %all-to-all-start.3) | async-done | bytes 524320 | tf_op jit(solution)/shard_map/all_to_all | solution.py:109
  342.1 9.1 %all-to-all-start.4 = ((f32[16,64,256]{2,0,1:T(8,128)}), f32[16,64,256]{2,0,1:T(8,128)S(1)}, u32[]{:S(2)}, u32[]{:S(2)}) async-start(f32[16,64,256]{2,0,1:T(8,128)} %bitcast.121), calls=%async_computation.4 | async-start | bytes 2097152 | tf_op jit(solution)/shard_map/all_to_all | solution.py:116
  351.6 2.9 fusion.2
  355.4 12.2 %all-to-all-done.4 = f32[16,64,256]{2,0,1:T(8,128)S(1)} async-done(((f32[16,64,256]{2,0,1:T(8,128)}), f32[16,64,256]{2,0,1:T(8,128)S(1)}, u32[]{:S(2)}, u32[]{:S(2)}) %all-to-all-start.4) | async-done | bytes 1048608 | tf_op jit(solution)/shard_map/all_to_all | solution.py:116
  368.2 1.6 copy.113
  (283 shorter events, 84.1 us)
Async XLA Ops:
  0.6 139.3 %copy-start = (bf16[256,160]{0,1:T(8,128)(2,1)S(1)}, bf16[256,160]{0,1:T(8,128)(2,1)}, u32[]{:S(2)}) copy-start(bf16[256,160]{0,1:T(8,128)(2,1)} %param.24) | copy-start | bytes 245764
  0.6 20.3 %copy-start.3 = (f32[8,16,2048]{2,1,0:T(8,128)S(1)}, f32[8,16,2048]{2,1,0:T(8,128)}, u32[]{:S(2)}) copy-start(f32[8,16,2048]{2,1,0:T(8,128)} %param.30) | copy-start | bytes 3145732
  8.6 17.1 %copy-start.2 = (bf16[8,16,1024]{2,1,0:T(8,128)(2,1)S(1)}, bf16[8,16,1024]{2,1,0:T(8,128)(2,1)}, u32[]{:S(2)}) copy-start(bf16[8,16,1024]{2,1,0:T(8,128)(2,1)} %param.19) | copy-start | bytes 786436
  8.6 17.4 %copy-start.4 = (f32[1024]{0:T(1024)S(1)}, f32[1024]{0:T(1024)}, u32[]{:S(2)}) copy-start(f32[1024]{0:T(1024)} %param.20) | copy-start | bytes 12292
  13.7 47.4 %all-to-all-start.1 = ((f32[8,1,6144]{2,1,0:T(1,128)}), f32[8,1,6144]{2,1,0:T(1,128)S(1)}, u32[]{:S(2)}, u32[]{:S(2)}) async-start(f32[8,1,6144]{2,1,0:T(1,128)} %reshape.188), calls=%async_computation.1 | async-start | bytes 393216 | tf_op jit(solution)/shard_map/all_to_all | solution.py:44
  52.9 8.2 %copy-start.12 = (s32[64]{0:T(128)S(1)}, s32[64]{0:T(128)}, u32[]{:S(2)}) copy-start(s32[64]{0:T(128)} %param.33) | copy-start | bytes 772
  52.9 14.3 %copy-start.13 = (s32[64]{0:T(128)S(1)}, s32[64]{0:T(128)}, u32[]{:S(2)}) copy-start(s32[64]{0:T(128)} %param.32) | copy-start | bytes 772
  52.9 25.7 %copy-start.9 = (s32[64]{0:T(128)S(1)}, s32[64]{0:T(128)}, u32[]{:S(2)}) copy-start(s32[64]{0:T(128)} %param.35) | copy-start | bytes 772
  52.9 25.9 %copy-start.6 = (f32[4,256]{1,0:T(4,128)S(1)}, f32[4,256]{1,0:T(4,128)}, u32[]{:S(2)}) copy-start(f32[4,256]{1,0:T(4,128)} %param.22) | copy-start | bytes 12292
  52.9 25.9 %copy-start.5 = (f32[16,256]{1,0:T(8,128)S(1)}, f32[16,256]{1,0:T(8,128)}, u32[]{:S(2)}) copy-start(f32[16,256]{1,0:T(8,128)} %param.27) | copy-start | bytes 49156
  61.1 31.4 %all-to-all-start = ((f32[8,1,32768]{2,1,0:T(1,128)}), f32[8,1,32768]{2,1,0:T(1,128)S(1)}, u32[]{:S(2)}, u32[]{:S(2)}) async-start(f32[8,1,32768]{2,1,0:T(1,128)} %reshape.184), calls=%async_computation | async-start | bytes 2097152 | tf_op jit(solution)/shard_map/all_to_all | solution.py:43
  92.5 29.4 %all-to-all-start.2 = ((bf16[8,2,32768]{2,1,0:T(2,128)(2,1)}), bf16[8,2,32768]{2,1,0:T(2,128)(2,1)S(1)}, u32[]{:S(2)}, u32[]{:S(2)}) async-start(bf16[8,2,32768]{2,1,0:T(2,128)(2,1)} %reshape.186), calls=%async_computation.2 | async-start | bytes 2097152 | tf_op jit(solution)/shard_map/all_to_all | solution.py:50
  112.4 27.0 %copy-start.7 = (f32[256]{0:T(256)S(1)}, f32[256]{0:T(256)}, u32[]{:S(2)}) copy-start(f32[256]{0:T(256)} %param.23) | copy-start | bytes 3076
  129.5 55.2 %copy-start.10 = (bf16[128,256]{1,0:T(8,128)(2,1)S(1)}, bf16[128,256]{1,0:T(8,128)(2,1)}, u32[]{:S(2)}) copy-start(bf16[128,256]{1,0:T(8,128)(2,1)} %param.25) | copy-start | bytes 196612
  129.5 55.2 %copy-start.11 = (f32[256]{0:T(256)S(1)}, f32[256]{0:T(256)}, u32[]{:S(2)}) copy-start(f32[256]{0:T(256)} %param.26) | copy-start | bytes 3076
  138.4 1.0 copy-start.1
  138.4 52.8 %copy-start.14 = (s32[64]{0:T(128)S(1)}, s32[64]{0:T(128)}, u32[]{:S(2)}) copy-start(s32[64]{0:T(128)} %param.34) | copy-start | bytes 772
  191.2 134.3 %copy-start.8 = (f32[256]{0:T(256)S(1)}, f32[256]{0:T(256)}, u32[]{:S(2)}) copy-start(f32[256]{0:T(256)} %param.28) | copy-start | bytes 3076
  328.1 14.0 %all-to-all-start.3 = ((bf16[16,64,256]{2,0,1:T(8,128)(2,1)}), bf16[16,64,256]{2,0,1:T(8,128)(2,1)S(1)}, u32[]{:S(2)}, u32[]{:S(2)}) async-start(bf16[16,64,256]{2,0,1:T(8,128)(2,1)} %copy.108), calls=%async_computation.3 | async-start | bytes 1048576 | tf_op jit(solution)/shard_map/all_to_all | solution.py:109
  342.1 25.5 %all-to-all-start.4 = ((f32[16,64,256]{2,0,1:T(8,128)}), f32[16,64,256]{2,0,1:T(8,128)S(1)}, u32[]{:S(2)}, u32[]{:S(2)}) async-start(f32[16,64,256]{2,0,1:T(8,128)} %bitcast.121), calls=%async_computation.4 | async-start | bytes 2097152 | tf_op jit(solution)/shard_map/all_to_all | solution.py:116
where the time goes:
time: 372 us; the launch traced here: 370 us
  local copies, waits for them, and re-layouts  191 us (51%)
  other arithmetic  47.8 us (13%)
  blocking collectives  43.6 us (12%)
  waiting for transfers between devices  33.9 us (9%)
  starting transfers between devices  29.5 us (8%)
  loops' own time  12.3 us (3%)
  matrix products  10.8 us (3%)
    unnamed x47, local copies, waits for them, and re-layouts  70.4 us
    psum x1, blocking collectives, on_device(): mixed_rows = lax.psum(partial_value, 'req').astype(jnp.bfloat16)  43.6 us
    dynamic_update_slice x16, local copies, waits for them, and re-layouts, on_device(): lax.scan(advance, (start_flat, start_flat), sliced)  31.1 us
    while x48, local copies, waits for them, and re-layouts  29.4 us
    dynamic_slice x16, other arithmetic, on_device(): lax.scan(advance, (start_flat, start_flat), sliced)  20.9 us
    reduce_sum x16, other arithmetic, advance(): result = jnp.sum(spread(step_c) * current, axis=0)  14.9 us
    another operation x1, loops' own time, on_device(): lax.scan(advance, (start_flat, start_flat), sliced)  12.3 us
    all_to_all x1, waiting for transfers between devices, on_device(): lax.all_to_all(chosen.reshape(state_size, all_reqs, channels), 'req', spl...  12.2 us
  transfers between devices with their start and end apart: 5, of which 4 were waited for; matrix products, arithmetic and copies ran while one was open for 23% of the time, Pallas kernels for 0%

commit v1 on v0

--- a/solution.py
+++ b/solution.py
@@ -4,6 +4,17 @@
 from jax.sharding import PartitionSpec as P
 
 EPS = 1e-05
+
+
+def in_blocks(array, dim, size):
+    before, after = (array.shape[:dim], array.shape[dim + 1 :])
+    return jnp.moveaxis(array.reshape(*before, size, -1, *after), dim, 0)
+
+
+def joined_along(blocks, dim):
+    blocks = jnp.moveaxis(blocks, 0, dim)
+    shape = blocks.shape
+    return blocks.reshape(*shape[:dim], shape[dim] * shape[dim + 1], *shape[dim + 2 :])
 
 
 def rms_normed(values_in, norm_gain):
@@ -47,7 +58,15 @@
     normed = rms_normed(token_major, norm_gain)
     projected = jnp.dot(normed, in_weight, preferred_element_type=jnp.float32).astype(jnp.bfloat16)
     projected = jnp.moveaxis(projected.reshape(draft_len, local_reqs, 2, inner_width), 2, 0)
-    grouped = lax.all_to_all(projected, "req", split_axis=3, concat_axis=2, tiled=True)
+    devices, here = (lax.axis_size("req"), lax.axis_index("req"))
+    parts = in_blocks(projected, 3, devices)
+    filled = parts
+    for step in range(1, devices):
+        target, source = ((here + step) % devices, (here - step) % devices)
+        sent = lax.dynamic_index_in_dim(parts, target, 0)
+        received = lax.ppermute(sent, "req", [(i, (i + step) % devices) for i in range(devices)])
+        filled = lax.dynamic_update_slice_in_dim(filled, received, source, axis=0)
+    grouped = joined_along(filled, 2)
     all_reqs = grouped.shape[2]
     inner_part = grouped[0]
     gate_part = grouped[1]

time: 372 us -> 326 us (0.88)
  local copies, waits for them, and re-layouts: 191 us -> 146 us
  waiting for transfers between devices: 33.9 us -> 23.1 us
  starting transfers between devices: 29.5 us -> 37.5 us
    unnamed x47 -> x44, local copies, waits for them, and re-layouts: 70.4 us -> 43 us
    ppermute x0 -> x7, starting transfers between devices: none -> 16.4 us  [on_device(): lax.ppermute(sent, 'req', [(i, (i + step) % devices) for i in range(devic...]
    all_to_all x1 -> x0, waiting for transfers between devices: 9.5 us -> none  [on_device(): lax.all_to_all(projected, 'req', split_axis=3, concat_axis=2, tiled=True)]
    all_to_all x1 -> x0, local copies, waits for them, and re-layouts: 8.9 us -> none  [on_device(): lax.all_to_all(projected, 'req', split_axis=3, concat_axis=2, tiled=True)]
    reshape x1, local copies, waits for them, and re-layouts: 8.85 us -> 0.1 us  [in_blocks(): return jnp.moveaxis(array.reshape(*before, size, -1, *after), dim, 0)]
    all_to_all x1, starting transfers between devices: 7.25 us -> 3.39 us  [on_device(): lax.all_to_all(edge_lead, 'req', split_axis=2, concat_axis=1, tiled=True)]
    all_to_all x1 -> x0, starting transfers between devices: 3.74 us -> none  [on_device(): lax.all_to_all(projected, 'req', split_axis=3, concat_axis=2, tiled=True)]
  transfers between devices with their start and end apart: 5 -> 11, of which waited for: 4 -> 3; matrix products, arithmetic and copies ran while one was open for 23% -> 17% of each run, Pallas kernels for 0% -> 0%
where the time goes in v1:
time: 326 us; the launch traced here: 325 us
  local copies, waits for them, and re-layouts  146 us (45%)
  other arithmetic  49.2 us (15%)
  blocking collectives  46.1 us (14%)
  starting transfers between devices  37.5 us (12%)
  waiting for transfers between devices  23.1 us (7%)
  loops' own time  11.8 us (4%)
  matrix products  9.02 us (3%)
    psum x1, blocking collectives, on_device(): mixed_rows = lax.psum(partial_value, 'req').astype(jnp.bfloat16)  46.1 us
    unnamed x44, local copies, waits for them, and re-layouts  43 us
    dynamic_update_slice x16, local copies, waits for them, and re-layouts, on_device(): lax.scan(advance, (start_flat, start_flat), sliced)  31.1 us
    while x48, local copies, waits for them, and re-layouts  29.4 us
    dynamic_slice x16, other arithmetic, on_device(): lax.scan(advance, (start_flat, start_flat), sliced)  20.9 us
    ppermute x7, starting transfers between devices, on_device(): lax.ppermute(sent, 'req', [(i, (i + step) % devices) for i in range(devic...  16.4 us
    reduce_sum x16, other arithmetic, advance(): result = jnp.sum(spread(step_c) * current, axis=0)  14.9 us
    all_to_all x1, waiting for transfers between devices, on_device(): lax.all_to_all(chosen.reshape(state_size, all_reqs, channels), 'req', spl...  12.1 us
  transfers between devices with their start and end apart: 11, of which 3 were waited for; matrix products, arithmetic and copies ran while one was open for 17% of the time, Pallas kernels for 0%

profile of v1, /device:TPU:0, one launch (start us, length us, event | category | flops | bytes accessed | tf_op | source)
XLA Modules:
  0.0 324.6 jit_solution(671944238314011705)
XLA Ops:
  2.1 4.9 %convolution_convert_fusion = bf16[128,4096]{1,0:T(8,128)(2,1)S(1)} fusion(bf16[1024,4096]{1,0:T(8,128)(2,1)} %param.21, f32[1024]{0:T(1024)} %param.20, f32[128]{0:T(128)S(1)} %rsqrt.12, bf16[8,16,1024]{2,1,0:T(8,128)(2,1)} %param.19), kind=kOutput, calls=%fused_computation.11 | convolution fusion | flops 1074790400 | bytes 9703936 | tf_op jit(solution)/shard_map/dot_general | solution.py:59
  7.8 2.9 collective-permute-start
  11.4 1.6 collective-permute-start.1
  13.0 2.6 collective-permute-start.2
  16.9 2.7 collective-permute-start.4
  19.6 2.7 copy.92
  22.3 3.9 %bitcast_bitcast_fusion.1 = f32[2048,3,8]{2,1,0:T(4,128)} fusion(f32[8,3,2048]{0,1,2:T(4,128)} %copy.92), kind=kLoop, calls=%fused_computation.93 | loop fusion | bytes 393216
  26.2 5.2 %reshape.198 = f32[8,1,6144]{2,1,0:T(1,128)} reshape(f32[2048,3,8]{2,1,0:T(4,128)} %bitcast_bitcast_fusion.1) | data formatting | bytes 393216
  31.4 3.4 %all-to-all-start.1 = ((f32[8,1,6144]{2,1,0:T(1,128)}), f32[8,1,6144]{2,1,0:T(1,128)S(1)}, u32[]{:S(2)}, u32[]{:S(2)}) async-start(f32[8,1,6144]{2,1,0:T(1,128)} %reshape.198), calls=%async_computation.1 | async-start | bytes 393216 | tf_op jit(solution)/shard_map/all_to_all | solution.py:55
  34.8 4.6 %copy.86 = f32[8,16,2048]{1,0,2:T(8,128)} copy(f32[8,16,2048]{2,1,0:T(8,128)S(1)} %copy-done.3) | data formatting | bytes 2097152 | tf_op args[11]
  39.5 5.8 %bitcast_bitcast_fusion = f32[2048,8,16]{2,1,0:T(8,128)} fusion(f32[8,16,2048]{1,0,2:T(8,128)} %copy.86), kind=kLoop, calls=%fused_computation.92 | loop fusion | bytes 2097152
  45.8 8.1 %reshape.196 = f32[8,1,32768]{2,1,0:T(1,128)} reshape(f32[2048,8,16]{2,1,0:T(8,128)} %bitcast_bitcast_fusion) | data formatting | bytes 2097152
  54.2 3.8 %collective-permute-start.5 = (bf16[1,2,16,8,256]{4,3,0,2,1:T(8,128)(2,1)S(1)}, bf16[1,2,16,8,256]{4,3,0,2,1:T(8,128)(2,1)S(1)}, u32[]{:S(2)}, u32[]{:S(2)}) collective-permute-start(bf16[1,2,16,8,256]{4,3,0,2,1:T(8,128)(2,1)S(1)} %bitcast.207), channel_id=1, source_target_pairs={{0,24},{4,28},{8,0},{12,4},{16,8},{20,12},{24,16},{28,20},{1,25},{... | collective-permute-start | bytes 393224 | tf_op jit(solution)/shard_map/ppermute | solution.py:67
  58.9 1.5 collective-permute-start.6
  62.4 1.6 collective-permute-done.6
  64.1 5.4 %all-to-all-start = ((f32[8,1,32768]{2,1,0:T(1,128)}), f32[8,1,32768]{2,1,0:T(1,128)}, u32[]{:S(2)}, u32[]{:S(2)}) async-start(f32[8,1,32768]{2,1,0:T(1,128)} %reshape.196), calls=%async_computation | async-start | bytes 2097152 | tf_op jit(solution)/shard_map/all_to_all | solution.py:54
  71.2 4.7 %reshape.199 = f32[2048,3,8]{2,1,0:T(4,128)} reshape(f32[8,6144]{1,0:T(8,128)S(1)} %reduce.3) | data formatting | bytes 393216
  75.8 3.5 %copy.93 = f32[3,8,8,256]{3,0,1,2:T(4,128)S(1)} copy(f32[3,8,8,256]{1,0,3,2:T(4,128)} %bitcast.178) | data formatting | bytes 393216 | tf_op jit(solution)/shard_map/all_to_all | solution.py:55
  81.1 46.1 %all-reduce.1 = bf16[1024,160]{0,1:T(8,128)(2,1)S(1)} all-reduce(f32[1024,160]{0,1:T(8,128)S(1)} %fusion.29), channel_id=1, replica_groups=mesh['req'=8,'grp'=4] {'req'}, use_global_device_ids=true, to_apply=%region_1.2 | all-reduce | flops 163840 | bytes 983040 | tf_op jit(solution)/shard_map/psum | solution.py:86
  129.2 1.3 copy.124
  130.7 4.4 %reduce.2 = f32[8,32768]{1,0:T(8,128)S(1)} reduce(f32[8,1,32768]{2,1,0:T(1,128)} %all-to-all-done, f32[]{:T(128)} %broadcast.103), dimensions={1}, to_apply=%all_to_all.50.reduce_sub_computation | reduce | bytes 2097156 | tf_op jit(solution)/shard_map/all_to_all | solution.py:54
  135.0 6.0 %reshape.197 = f32[2048,8,16]{2,1,0:T(8,128)} reshape(f32[8,32768]{1,0:T(8,128)S(1)} %reduce.2) | data formatting | bytes 2097152
  141.0 5.4 %copy.88 = f32[16,8,8,256]{3,2,1,0:T(8,128)S(1)} copy(f32[16,8,8,256]{0,2,3,1:T(8,128)} %bitcast.177) | data formatting | bytes 2097152 | tf_op jit(solution)/shard_map/all_to_all | solution.py:54
  148.0 131.0 %while.15 = (s32[]{:T(128)}, f32[16,16384]{1,0:T(8,128)S(1)}, f32[16,16384]{1,0:T(8,128)S(1)}, f32[16,16384]{1,0:T(8,128)}, f32[16,16384]{1,0:T(8,128)}, /*index...) while((s32[]{:T(128)}, f32[16,16384]{1,0:T(8,128)S(1)}, ...), condition=%wide.region_4.5_spmd.clone, body=%wide.region_2.4_spmd.clone.sunk | while | flops 1835075 | bytes 18522676 | solution.py:123
  149.9 1.3 constant_dynamic-slice_fusion.13
  154.5 1.9 dynamic_update_slice.41
  158.1 1.3 constant_dynamic-slice_fusion.13
  162.7 1.9 dynamic_update_slice.41
  166.3 1.3 constant_dynamic-slice_fusion.13
  170.8 1.9 dynamic_update_slice.41
  174.4 1.3 constant_dynamic-slice_fusion.13
  179.0 1.9 dynamic_update_slice.41
  182.6 1.3 constant_dynamic-slice_fusion.13
  187.1 1.9 dynamic_update_slice.41
  190.7 1.3 constant_dynamic-slice_fusion.13
  195.3 1.9 dynamic_update_slice.41
  198.9 1.3 constant_dynamic-slice_fusion.13
  203.5 1.9 dynamic_update_slice.41
  207.1 1.3 constant_dynamic-slice_fusion.13
  211.6 1.9 dynamic_update_slice.41
  215.2 1.3 constant_dynamic-slice_fusion.13
  219.8 1.9 dynamic_update_slice.41
  223.4 1.3 constant_dynamic-slice_fusion.13
  228.0 1.9 dynamic_update_slice.41
  231.6 1.3 constant_dynamic-slice_fusion.13
  236.2 1.9 dynamic_update_slice.41
  239.8 1.3 constant_dynamic-slice_fusion.13
  244.3 1.9 dynamic_update_slice.41
  247.9 1.3 constant_dynamic-slice_fusion.13
  252.5 1.9 dynamic_update_slice.41
  256.1 1.3 constant_dynamic-slice_fusion.13
  260.7 1.9 dynamic_update_slice.41
  264.3 1.3 constant_dynamic-slice_fusion.13
  268.9 1.9 dynamic_update_slice.41
  272.5 1.3 constant_dynamic-slice_fusion.13
  277.0 1.9 dynamic_update_slice.41
  279.0 1.5 copy.125
  280.5 1.5 fusion.16
  283.1 3.5 %all-to-all-start.2 = ((bf16[16,64,256]{2,0,1:T(8,128)(2,1)}), bf16[16,64,256]{2,0,1:T(8,128)(2,1)S(1)}, u32[]{:S(2)}, u32[]{:S(2)}) async-start(bf16[16,64,256]{2,0,1:T(8,128)(2,1)} %copy.106), calls=%async_computation.2 | async-start | bytes 1048576 | tf_op jit(solution)/shard_map/all_to_all | solution.py:128
  287.8 9.4 %all-to-all-done.2 = bf16[16,64,256]{2,0,1:T(8,128)(2,1)S(1)} async-done(((bf16[16,64,256]{2,0,1:T(8,128)(2,1)}), bf16[16,64,256]{2,0,1:T(8,128)(2,1)S(1)}, u32[]{:S(2)}, u32[]{:S(2)}) %all-to-all-start.2) | async-done | bytes 524320 | tf_op jit(solution)/shard_map/all_to_all | solution.py:128
  297.2 8.8 %all-to-all-start.3 = ((f32[16,64,256]{2,0,1:T(8,128)}), f32[16,64,256]{2,0,1:T(8,128)S(1)}, u32[]{:S(2)}, u32[]{:S(2)}) async-start(f32[16,64,256]{2,0,1:T(8,128)} %bitcast.135), calls=%async_computation.3 | async-start | bytes 2097152 | tf_op jit(solution)/shard_map/all_to_all | solution.py:135
  306.4 3.0 fusion.2
  310.3 12.1 %all-to-all-done.3 = f32[16,64,256]{2,0,1:T(8,128)S(1)} async-done(((f32[16,64,256]{2,0,1:T(8,128)}), f32[16,64,256]{2,0,1:T(8,128)S(1)}, u32[]{:S(2)}, u32[]{:S(2)}) %all-to-all-start.3) | async-done | bytes 1048608 | tf_op jit(solution)/shard_map/all_to_all | solution.py:135
  323.0 1.6 copy.111
  (305 shorter events, 85.9 us)
Async XLA Ops:
  0.6 80.2 %copy-start = (bf16[256,160]{0,1:T(8,128)(2,1)S(1)}, bf16[256,160]{0,1:T(8,128)(2,1)}, u32[]{:S(2)}) copy-start(bf16[256,160]{0,1:T(8,128)(2,1)} %param.24) | copy-start | bytes 245764
  2.0 17.6 %copy-start.4 = (bf16[8,3,2048]{2,0,1:T(8,128)(2,1)S(1)}, bf16[8,3,2048]{2,0,1:T(8,128)(2,1)}, u32[]{:S(2)}) copy-start(bf16[8,3,2048]{2,0,1:T(8,128)(2,1)} %param.31) | copy-start | bytes 294916
  7.8 46.4 %collective-permute-start = (bf16[1,2,16,8,256]{4,3,0,2,1:T(8,128)(2,1)}, bf16[1,2,16,8,256]{4,3,0,2,1:T(8,128)(2,1)}, u32[]{:S(2)}, u32[]{:S(2)}) collective-permute-start(bf16[1,2,16,8,256]{4,3,0,2,1:T(8,128)(2,1)} %bitcast.145), channel_id=1, source_target_pairs={{0,4},{4,8},{8,12},{12,16},{16,20},{20,24},{24,28},{28,0},{1,5},{5... | collective-permute-start | bytes 393224 | tf_op jit(solution)/shard_map/ppermute | solution.py:67
  11.4 47.5 %collective-permute-start.1 = (bf16[1,2,16,8,256]{4,3,0,2,1:T(8,128)(2,1)}, bf16[1,2,16,8,256]{4,3,0,2,1:T(8,128)(2,1)}, u32[]{:S(2)}, u32[]{:S(2)}) collective-permute-start(bf16[1,2,16,8,256]{4,3,0,2,1:T(8,128)(2,1)} %bitcast.144), channel_id=1, source_target_pairs={{0,8},{4,12},{8,16},{12,20},{16,24},{20,28},{24,0},{28,4},{1,9},{5... | collective-permute-start | bytes 393224 | tf_op jit(solution)/shard_map/ppermute | solution.py:67
  13.0 48.4 %collective-permute-start.2 = (bf16[1,2,16,8,256]{4,3,0,2,1:T(8,128)(2,1)S(1)}, bf16[1,2,16,8,256]{4,3,0,2,1:T(8,128)(2,1)}, u32[]{:S(2)}, u32[]{:S(2)}) collective-permute-start(bf16[1,2,16,8,256]{4,3,0,2,1:T(8,128)(2,1)S(1)} %bitcast.205), channel_id=1, source_target_pairs={{0,12},{4,16},{8,20},{12,24},{16,28},{20,0},{24,4},{28,8},{1,13},{... | collective-permute-start | bytes 393224 | tf_op jit(solution)/shard_map/ppermute | solution.py:67
  15.6 46.7 %collective-permute-start.3 = (bf16[1,2,16,8,256]{4,3,0,2,1:T(8,128)(2,1)S(1)}, bf16[1,2,16,8,256]{4,3,0,2,1:T(8,128)(2,1)S(1)}, u32[]{:S(2)}, u32[]{:S(2)}) collective-permute-start(bf16[1,2,16,8,256]{4,3,0,2,1:T(8,128)(2,1)S(1)} %bitcast.204), channel_id=1, source_target_pairs={{0,16},{4,20},{8,24},{12,28},{16,0},{20,4},{24,8},{28,12},{1,17},{... | collective-permute-start | bytes 393224 | tf_op jit(solution)/shard_map/ppermute | solution.py:67
  16.9 45.4 %collective-permute-start.4 = (bf16[1,2,16,8,256]{4,3,0,2,1:T(8,128)(2,1)S(1)}, bf16[1,2,16,8,256]{4,3,0,2,1:T(8,128)(2,1)S(1)}, u32[]{:S(2)}, u32[]{:S(2)}) collective-permute-start(bf16[1,2,16,8,256]{4,3,0,2,1:T(8,128)(2,1)S(1)} %bitcast.203), channel_id=1, source_target_pairs={{0,20},{4,24},{8,28},{12,0},{16,4},{20,8},{24,12},{28,16},{1,21},{... | collective-permute-start | bytes 393224 | tf_op jit(solution)/shard_map/ppermute | solution.py:67
  26.2 8.6 %copy-start.3 = (f32[8,16,2048]{2,1,0:T(8,128)S(1)}, f32[8,16,2048]{2,1,0:T(8,128)}, u32[]{:S(2)}) copy-start(f32[8,16,2048]{2,1,0:T(8,128)} %param.30) | copy-start | bytes 3145732
  31.4 32.7 %all-to-all-start.1 = ((f32[8,1,6144]{2,1,0:T(1,128)}), f32[8,1,6144]{2,1,0:T(1,128)S(1)}, u32[]{:S(2)}, u32[]{:S(2)}) async-start(f32[8,1,6144]{2,1,0:T(1,128)} %reshape.198), calls=%async_computation.1 | async-start | bytes 393216 | tf_op jit(solution)/shard_map/all_to_all | solution.py:55
  39.5 5.8 %copy-start.9 = (s32[64]{0:T(128)S(1)}, s32[64]{0:T(128)}, u32[]{:S(2)}) copy-start(s32[64]{0:T(128)} %param.33) | copy-start | bytes 772
  39.5 5.9 %copy-start.11 = (s32[64]{0:T(128)S(1)}, s32[64]{0:T(128)}, u32[]{:S(2)}) copy-start(s32[64]{0:T(128)} %param.32) | copy-start | bytes 772
  39.5 5.9 %copy-start.6 = (f32[4,256]{1,0:T(4,128)S(1)}, f32[4,256]{1,0:T(4,128)}, u32[]{:S(2)}) copy-start(f32[4,256]{1,0:T(4,128)} %param.22) | copy-start | bytes 12292
  39.5 5.9 %copy-start.5 = (f32[16,256]{1,0:T(8,128)S(1)}, f32[16,256]{1,0:T(8,128)}, u32[]{:S(2)}) copy-start(f32[16,256]{1,0:T(8,128)} %param.27) | copy-start | bytes 49156
  39.5 6.0 %copy-start.10 = (s32[64]{0:T(128)S(1)}, s32[64]{0:T(128)}, u32[]{:S(2)}) copy-start(s32[64]{0:T(128)} %param.35) | copy-start | bytes 772
  54.2 8.1 %collective-permute-start.5 = (bf16[1,2,16,8,256]{4,3,0,2,1:T(8,128)(2,1)S(1)}, bf16[1,2,16,8,256]{4,3,0,2,1:T(8,128)(2,1)S(1)}, u32[]{:S(2)}, u32[]{:S(2)}) collective-permute-start(bf16[1,2,16,8,256]{4,3,0,2,1:T(8,128)(2,1)S(1)} %bitcast.207), channel_id=1, source_target_pairs={{0,24},{4,28},{8,0},{12,4},{16,8},{20,12},{24,16},{28,20},{1,25},{... | collective-permute-start | bytes 393224 | tf_op jit(solution)/shard_map/ppermute | solution.py:67
  58.9 5.0 %collective-permute-start.6 = (bf16[1,2,16,8,256]{4,3,0,2,1:T(8,128)(2,1)S(1)}, bf16[1,2,16,8,256]{4,3,0,2,1:T(8,128)(2,1)S(1)}, u32[]{:S(2)}, u32[]{:S(2)}) collective-permute-start(bf16[1,2,16,8,256]{4,3,0,2,1:T(8,128)(2,1)S(1)} %bitcast.206), channel_id=1, source_target_pairs={{0,28},{4,0},{8,4},{12,8},{16,12},{20,16},{24,20},{28,24},{1,29},{... | collective-permute-start | bytes 393224 | tf_op jit(solution)/shard_map/ppermute | solution.py:67
  64.0 11.9 %copy-start.2 = (bf16[8,2,16,8,256]{4,3,0,2,1:T(8,128)(2,1)}, bf16[8,2,16,8,256]{4,3,0,2,1:T(8,128)(2,1)S(1)}, u32[]{:S(2)}) copy-start(bf16[8,2,16,8,256]{4,3,0,2,1:T(8,128)(2,1)S(1)} %constant_dynamic-update-slice_fusion) | copy-start | bytes 3145732
  64.1 66.5 %all-to-all-start = ((f32[8,1,32768]{2,1,0:T(1,128)}), f32[8,1,32768]{2,1,0:T(1,128)}, u32[]{:S(2)}, u32[]{:S(2)}) async-start(f32[8,1,32768]{2,1,0:T(1,128)} %reshape.196), calls=%async_computation | async-start | bytes 2097152 | tf_op jit(solution)/shard_map/all_to_all | solution.py:54
  71.2 9.2 %copy-start.7 = (f32[256]{0:T(256)S(1)}, f32[256]{0:T(256)}, u32[]{:S(2)}) copy-start(f32[256]{0:T(256)} %param.23) | copy-start | bytes 3076
  75.8 51.4 %copy-start.12 = (bf16[128,256]{1,0:T(8,128)(2,1)S(1)}, bf16[128,256]{1,0:T(8,128)(2,1)}, u32[]{:S(2)}) copy-start(bf16[128,256]{1,0:T(8,128)(2,1)} %param.25) | copy-start | bytes 196612
  75.8 51.4 %copy-start.13 = (f32[256]{0:T(256)S(1)}, f32[256]{0:T(256)}, u32[]{:S(2)}) copy-start(f32[256]{0:T(256)} %param.26) | copy-start | bytes 3076
  147.0 1.0 copy-start.14
  148.0 132.5 %copy-start.8 = (f32[256]{0:T(256)S(1)}, f32[256]{0:T(256)}, u32[]{:S(2)}) copy-start(f32[256]{0:T(256)} %param.28) | copy-start | bytes 3076
  283.1 14.0 %all-to-all-start.2 = ((bf16[16,64,256]{2,0,1:T(8,128)(2,1)}), bf16[16,64,256]{2,0,1:T(8,128)(2,1)S(1)}, u32[]{:S(2)}, u32[]{:S(2)}) async-start(bf16[16,64,256]{2,0,1:T(8,128)(2,1)} %copy.106), calls=%async_computation.2 | async-start | bytes 1048576 | tf_op jit(solution)/shard_map/all_to_all | solution.py:128
  297.2 25.2 %all-to-all-start.3 = ((f32[16,64,256]{2,0,1:T(8,128)}), f32[16,64,256]{2,0,1:T(8,128)S(1)}, u32[]{:S(2)}, u32[]{:S(2)}) async-start(f32[16,64,256]{2,0,1:T(8,128)} %bitcast.135), calls=%async_computation.3 | async-start | bytes 2097152 | tf_op jit(solution)/shard_map/all_to_all | solution.py:135
  306.4 18.2 %copy-start.1 = (bf16[256,160]{0,1:T(8,128)(2,1)S(1)}, bf16[256,160]{0,1:T(8,128)(2,1)}, u32[]{:S(2)}) copy-start(bf16[256,160]{0,1:T(8,128)(2,1)} %param.24) | copy-start | bytes 245764
